TPU v7x, 256 devices: a whole 4x4x8 slice. The times are simulated.
256 devices in a mesh: seq: 32 (over x_hi, z, core), tp: 8 (over y, x_lo).
Axes of the slice: x: 4 (x_hi: 2, x_lo: 2; x = x_hi * 2 + x_lo), y: 4, z: 8, core: 2. Of those that a mesh axis runs over, the one named last changes fastest.
Arguments:
- queries: bfloat16 [8, 4096, 4096], P('tp', 'seq'), may hold values from -9 to 9
- key_rows: bfloat16 [8, 4096, 4096], P('tp', 'seq'), may hold values from -6 to 6
- values: bfloat16 [8, 4096, 4096], P('tp', 'seq'), may hold values from -6 to 6
- upstream: bfloat16 [8, 4096, 4096], P(None, 'seq', 'tp'), may hold values from -6 to 6
- out_weight: bfloat16 [4096, 4096], P(None, 'tp'), may hold values from -0.09375 to 0.09375
- blocks: int32 [64, 4], replicated, may hold values from 0 to 63, as said below
Outputs:
- attended: bfloat16 [8, 4096, 4096], P('tp', 'seq')
- grad_queries: bfloat16 [8, 4096, 4096], P('tp', 'seq')
- grad_keys: bfloat16 [8, 4096, 4096], P('tp', 'seq')
- grad_values: bfloat16 [8, 4096, 4096], P('tp', 'seq')
- grad_weight: float32 [4096, 4096], P('seq', 'tp')
Inputs may be any that keep to these rules, and one draw needn't show every extreme that they name: Row a lists the blocks a - 1, a and a + 1 modulo 64, then one block 2 to 62 blocks after a modulo 64; no row names a block twice.
All inputs are finite; a program needn't handle non-finite values.
Results may differ from a plain program's by a relative error of at most 0.022.
Values may be sent and summed in bfloat16 or wider, within the bound.
A program may use at most 128 MiB of HBM per device.

v0:
```python
import math
import jax
import jax.numpy as jnp
from jax import lax
from jax.sharding import PartitionSpec as P

HD = 128
BLK = 64
NB = 4


def forward_head(query_rows, key_rows, value_rows, blocks):
    block_count = blocks.shape[0]
    factor = 1.0 / math.sqrt(HD)
    query_tiles = query_rows.reshape(block_count, BLK, HD)
    key_set = key_rows.reshape(block_count, BLK, HD)[blocks].reshape(block_count, NB * BLK, HD)
    value_set = value_rows.reshape(block_count, BLK, HD)[blocks].reshape(block_count, NB * BLK, HD)
    scores = (
        jnp.einsum("qid,qjd->qij", query_tiles, key_set, preferred_element_type=jnp.float32)
        * factor
    )
    row_max = jnp.max(scores, axis=-1, keepdims=True)
    shifted = jnp.exp(scores - row_max)
    soft_probs = shifted / jnp.sum(shifted, axis=-1, keepdims=True)
    probs_low = soft_probs.astype(jnp.bfloat16)
    context = jnp.einsum(
        "qij,qjd->qid", probs_low, value_set, preferred_element_type=jnp.float32
    ).astype(jnp.bfloat16)
    return (context, soft_probs, probs_low, key_set, value_set)


def backward_head(query_rows, grad_rows, blocks, saved):
    context, soft_probs, probs_low, key_set, value_set = saved
    block_count = blocks.shape[0]
    factor = 1.0 / math.sqrt(HD)
    query_tiles = query_rows.reshape(block_count, BLK, HD)
    grad_tiles = grad_rows.reshape(block_count, BLK, HD)
    row_delta = jnp.sum(
        grad_tiles.astype(jnp.float32) * context.astype(jnp.float32), axis=-1, keepdims=True
    )
    dprobs = jnp.einsum("qid,qjd->qij", grad_tiles, value_set, preferred_element_type=jnp.float32)
    dscores = (soft_probs * (dprobs - row_delta) * factor).astype(jnp.bfloat16)
    query_grad = jnp.einsum(
        "qij,qjd->qid", dscores, key_set, preferred_element_type=jnp.float32
    ).astype(jnp.bfloat16)
    flat_list = blocks.reshape(-1)
    key_parts = jnp.einsum(
        "qij,qid->qjd", dscores, query_tiles, preferred_element_type=jnp.float32
    ).reshape(block_count * NB, BLK, HD)
    value_parts = jnp.einsum(
        "qij,qid->qjd", probs_low, grad_tiles, preferred_element_type=jnp.float32
    ).reshape(block_count * NB, BLK, HD)
    key_grad = (
        jnp.zeros((block_count, BLK, HD), jnp.float32)
        .at[flat_list]
        .add(key_parts)
        .astype(jnp.bfloat16)
    )
    value_grad = (
        jnp.zeros((block_count, BLK, HD), jnp.float32)
        .at[flat_list]
        .add(value_parts)
        .astype(jnp.bfloat16)
    )
    return (query_grad, key_grad, value_grad)


def on_device(queries, key_rows, values, upstream, out_weight, blocks):
    head_queries, head_keys, head_values = (
        lax.all_to_all(queries, "seq", split_axis=2, concat_axis=1, tiled=True),
        lax.all_to_all(key_rows, "seq", split_axis=2, concat_axis=1, tiled=True),
        lax.all_to_all(values, "seq", split_axis=2, concat_axis=1, tiled=True),
    )
    length = head_queries.shape[1]
    count_heads = head_queries.shape[2] // HD

    def split_heads(array):
        return array.reshape(length, count_heads, HD).transpose(1, 0, 2)

    def join_heads(array):
        return (
            array.reshape(count_heads, length, HD)
            .transpose(1, 0, 2)
            .reshape(1, length, count_heads * HD)
        )

    grad_tokens = lax.psum_scatter(
        jnp.einsum("stc,dc->std", upstream, out_weight, preferred_element_type=jnp.float32).astype(
            jnp.bfloat16
        ),
        "tp",
        scatter_dimension=0,
        tiled=True,
    )
    grad_heads = lax.all_to_all(grad_tokens, "seq", split_axis=2, concat_axis=1, tiled=True)
    stacked = (
        split_heads(head_queries),
        split_heads(head_keys),
        split_heads(head_values),
        split_heads(grad_heads),
    )

    def both_one(packed):
        saved_one = forward_head(packed[0], packed[1], packed[2], blocks)
        return (saved_one[0],) + backward_head(packed[0], packed[3], blocks, saved_one)

    results = lax.map(both_one, stacked)
    attended, query_grad, key_grad, value_grad = (
        lax.all_to_all(join_heads(results[0]), "seq", split_axis=1, concat_axis=2, tiled=True),
        lax.all_to_all(join_heads(results[1]), "seq", split_axis=1, concat_axis=2, tiled=True),
        lax.all_to_all(join_heads(results[2]), "seq", split_axis=1, concat_axis=2, tiled=True),
        lax.all_to_all(join_heads(results[3]), "seq", split_axis=1, concat_axis=2, tiled=True),
    )
    every_sequence = lax.all_gather(attended, "tp", axis=0, tiled=True)
    grad_weight = lax.psum_scatter(
        jnp.einsum(
            "str,stc->rc", every_sequence, upstream, preferred_element_type=jnp.float32
        ).astype(jnp.bfloat16),
        "seq",
        scatter_dimension=0,
        tiled=True,
    ).astype(jnp.float32)
    return (attended, query_grad, key_grad, value_grad, grad_weight)


def solution(mesh):
    in_specs = (
        P("tp", "seq", None),
        P("tp", "seq", None),
        P("tp", "seq", None),
        P(None, "seq", "tp"),
        P(None, "tp"),
        P(),
    )
    out_specs = (
        P("tp", "seq", None),
        P("tp", "seq", None),
        P("tp", "seq", None),
        P("tp", "seq", None),
        P("seq", "tp"),
    )
    return jax.shard_map(
        on_device, mesh=mesh, in_specs=in_specs, out_specs=out_specs, check_vma=False
    )
```

profile of v0, /device:TPU:32, one launch (start us, length us, event | category | flops | bytes accessed | tf_op | source)
XLA Modules:
  0.0 871.2 jit_solution(8195947875667358401)
XLA Ops:
  22.9 23.4 %reduce.1 = bf16[4096,128]{1,0:T(8,128)(2,1)} reduce(bf16[4096,1,128]{2,1,0:T(2,128)(2,1)S(1)} %bitcast.130, bf16[]{:T(256)} %broadcast.81), dimensions={1}, to_apply=%bitcast.71.reduce_sub_computation | reduce | bytes 2097154
  48.4 11.9 %all-to-all-start.2 = ((bf16[32,2,8192]{2,1,0:T(2,128)(2,1)}), bf16[32,2,8192]{2,1,0:T(2,128)(2,1)}, u32[]{:S(2)}, u32[]{:S(2)}) async-start(bf16[32,2,8192]{2,1,0:T(2,128)(2,1)} %reshape.139), calls=%async_computation.2 | async-start | bytes 2097152 | tf_op jit(solution)/shard_map/all_to_all | solution.py:72
  65.3 23.4 %reduce.2 = bf16[4096,128]{1,0:T(8,128)(2,1)} reduce(bf16[4096,1,128]{2,1,0:T(2,128)(2,1)S(1)} %bitcast.136, bf16[]{:T(256)} %broadcast.81), dimensions={1}, to_apply=%bitcast.73.reduce_sub_computation | reduce | bytes 2097154
  105.8 23.4 %reduce.3 = bf16[4096,128]{1,0:T(8,128)(2,1)} reduce(bf16[4096,1,128]{2,1,0:T(2,128)(2,1)S(1)} %bitcast.137, bf16[]{:T(256)} %broadcast.81), dimensions={1}, to_apply=%bitcast.75.reduce_sub_computation | reduce | bytes 2097154
  131.4 10.1 %all-to-all-start.1 = ((bf16[32,2,8192]{2,1,0:T(2,128)(2,1)}), bf16[32,2,8192]{2,1,0:T(2,128)(2,1)}, u32[]{:S(2)}, u32[]{:S(2)}) async-start(bf16[32,2,8192]{2,1,0:T(2,128)(2,1)} %reshape.143), calls=%async_computation.1 | async-start | bytes 2097152 | tf_op jit(solution)/shard_map/all_to_all | solution.py:70
  141.5 84.0 %reduce-scatter.3.cloned.1.call-done = bf16[1,128,4096]{2,1,0:T(8,128)(2,1)} async-done(((bf16[8,128,4096]{2,1,0:T(8,128)(2,1)}), bf16[1,128,4096]{2,1,0:T(8,128)(2,1)}) %reduce-scatter.3.cloned.1.call-update) | async-done | bytes 1048592 | tf_op jit(solution)/shard_map/reduce_scatter | solution.py:87
  230.6 23.4 %reduce = bf16[4096,128]{1,0:T(8,128)(2,1)} reduce(bf16[4096,1,128]{2,1,0:T(2,128)(2,1)S(1)} %bitcast.132, bf16[]{:T(256)} %broadcast.81), dimensions={1}, to_apply=%bitcast.79.reduce_sub_computation | reduce | bytes 2097154
  313.9 12.7 %multiply_reduce_fusion = (f32[64,64]{1,0:T(8,128)S(1)}, bf16[64,64,128]{2,1,0:T(8,128)(2,1)S(1)}) fusion(bf16[64,64,128]{2,1,0:T(8,128)(2,1)} %bitcast.156, bf16[64,256,128]{2,1,0:T(8,128)(2,1)} %bitcast.149, f32[64,64]{1,0:T(8,128)S(1)} %get-tuple-element.65, f32[64,256,64]{1,2,0:T(8,128)} %copy-done.2), kind=kOutput, calls=%fused_computation.14 | convolution fusion | flops 276300032 | bytes 10518528 | tf_op jit(solution)/shard_map/while/body/eval_jaxpr/qij,qjd->qid/dot_general | solution.py:26
  326.6 17.5 %copy.116 = bf16[1,4096,128]{2,0,1:T(2,128)(2,1)} copy(bf16[1,4096,128]{2,1,0:T(8,128)(2,1)S(1)} %bitcast.155) | data formatting | bytes 2097152 | tf_op jit(solution)/shard_map/reshape;transpose;reshape | solution.py:84
  344.0 23.4 %reduce.4 = bf16[4096,128]{1,0:T(8,128)(2,1)S(1)} reduce(bf16[4096,1,128]{2,1,0:T(2,128)(2,1)} %bitcast.133, bf16[]{:T(256)} %broadcast.81), dimensions={1}, to_apply=%bitcast.113.reduce_sub_computation | reduce | bytes 2097154
  368.6 40.3 %all_to_all.132 = bf16[32,2,8192]{2,1,0:T(2,128)(2,1)S(1)} all-to-all(bf16[32,2,8192]{2,1,0:T(2,128)(2,1)} %reshape.145), channel_id=1, replica_groups=mesh['seq'=32,'tp'=8] {'seq'}, dimensions={0} | all-to-all | bytes 2097152 | tf_op jit(solution)/shard_map/all_to_all | solution.py:109
  425.2 158.5 %all-gather.2.cloned.1.call-done = bf16[8,128,4096]{2,1,0:T(8,128)(2,1)} async-done(((bf16[1,128,4096]{2,1,0:T(8,128)(2,1)}), bf16[8,128,4096]{2,1,0:T(8,128)(2,1)}) %all-gather.2.cloned.1.call-update) | async-done | bytes 8388624 | tf_op jit(solution)/shard_map/all_gather | solution.py:114
  597.2 17.0 %copy.115 = bf16[1,4096,128]{2,0,1:T(2,128)(2,1)} copy(bf16[1,4096,128]{2,1,0:T(8,128)(2,1)S(1)} %bitcast.138) | data formatting | bytes 2097152 | tf_op jit(solution)/shard_map/reshape;transpose;reshape | solution.py:84
  614.2 23.5 %reduce.5 = bf16[4096,128]{1,0:T(8,128)(2,1)S(1)} reduce(bf16[4096,1,128]{2,1,0:T(2,128)(2,1)} %bitcast.134, bf16[]{:T(256)} %broadcast.81), dimensions={1}, to_apply=%bitcast.112.reduce_sub_computation | reduce | bytes 2097154
  638.8 10.2 %all-to-all-start.5 = ((bf16[32,2,8192]{2,1,0:T(2,128)(2,1)}), bf16[32,2,8192]{2,1,0:T(2,128)(2,1)}, u32[]{:S(2)}, u32[]{:S(2)}) async-start(bf16[32,2,8192]{2,1,0:T(2,128)(2,1)} %reshape.149), calls=%async_computation.6 | async-start | bytes 2097152 | tf_op jit(solution)/shard_map/all_to_all | solution.py:110
  655.5 26.3 %scatter_fusion = f32[64,64,128]{2,1,0:T(8,128)S(1)} fusion(f32[64,64,128]{2,1,0:T(8,128)S(1)} %broadcast.50.clone, s32[256]{0:T(256)S(1)} %bitcast.159, f32[256,64,128]{2,1,0:T(8,128)} %bitcast.116), kind=kCustom, calls=%fused_computation.2 | custom fusion | flops 2097152 | bytes 25166848 | tf_op jit(solution)/shard_map/while/body/eval_jaxpr/scatter-add | solution.py:56
  682.0 16.7 %copy.114 = bf16[1,4096,128]{2,0,1:T(2,128)(2,1)S(1)} copy(bf16[1,4096,128]{2,1,0:T(8,128)(2,1)S(1)} %bitcast.139) | data formatting | bytes 2097152 | tf_op jit(solution)/shard_map/reshape;transpose;reshape | solution.py:84
  698.8 22.4 %reduce.6 = bf16[4096,128]{1,0:T(8,128)(2,1)S(1)} reduce(bf16[4096,1,128]{2,1,0:T(2,128)(2,1)S(1)} %bitcast.135, bf16[]{:T(256)} %broadcast.81), dimensions={1}, to_apply=%bitcast.111.reduce_sub_computation | reduce | bytes 2097154
  722.3 10.3 %all-to-all-start.6 = ((bf16[32,2,8192]{2,1,0:T(2,128)(2,1)}), bf16[32,2,8192]{2,1,0:T(2,128)(2,1)}, u32[]{:S(2)}, u32[]{:S(2)}) async-start(bf16[32,2,8192]{2,1,0:T(2,128)(2,1)} %reshape.151), calls=%async_computation.7 | async-start | bytes 2097152 | tf_op jit(solution)/shard_map/all_to_all | solution.py:111
  732.6 14.2 %fusion.10 = f32[64,256,128]{2,1,0:T(8,128)} fusion(bf16[64,64,128]{2,1,0:T(8,128)(2,1)S(1)} %bitcast.158, f32[64,64]{1,0:T(8,128)S(1)} %get-tuple-element.65, f32[64,256,64]{1,2,0:T(8,128)} %copy-done.2), kind=kOutput, calls=%fused_computation.24 | convolution fusion | flops 273682688 | bytes 13647872 | tf_op jit(solution)/shard_map/while/body/eval_jaxpr/qij,qid->qjd/dot_general | solution.py:50
  747.0 26.2 %scatter_fusion.1 = f32[64,64,128]{2,1,0:T(8,128)S(1)} fusion(f32[64,64,128]{2,1,0:T(8,128)S(1)} %broadcast.50.clone.1, s32[256]{0:T(256)S(1)} %bitcast.160, f32[256,64,128]{2,1,0:T(8,128)} %bitcast.129), kind=kCustom, calls=%fused_computation.3 | custom fusion | flops 2097152 | bytes 25166848 | tf_op jit(solution)/shard_map/while/body/eval_jaxpr/scatter-add | solution.py:62
  773.5 16.7 %copy.113 = bf16[1,4096,128]{2,0,1:T(2,128)(2,1)S(1)} copy(bf16[1,4096,128]{2,1,0:T(8,128)(2,1)S(1)} %bitcast.140) | data formatting | bytes 2097152 | tf_op jit(solution)/shard_map/reshape;transpose;reshape | solution.py:84
  790.2 22.4 %reduce.7 = bf16[4096,128]{1,0:T(8,128)(2,1)S(1)} reduce(bf16[4096,1,128]{2,1,0:T(2,128)(2,1)S(1)} %bitcast.131, bf16[]{:T(256)} %broadcast.81), dimensions={1}, to_apply=%bitcast.110.reduce_sub_computation | reduce | bytes 2097154
  836.5 17.7 %all-to-all-done.7 = bf16[32,2,8192]{2,1,0:T(2,128)(2,1)} async-done(((bf16[32,2,8192]{2,1,0:T(2,128)(2,1)}), bf16[32,2,8192]{2,1,0:T(2,128)(2,1)}, u32[]{:S(2)}, u32[]{:S(2)}) %all-to-all-start.7) | async-done | bytes 1048608 | tf_op jit(solution)/shard_map/all_to_all | solution.py:112
  (88 shorter events, 181.1 us)
Async XLA Ops:
  7.2 1.2 copy-start
  7.2 218.3 %reduce-scatter.3.cloned.1.call-start = ((), (), s32[]{:S(2)}) async-start(), calls=%async_computation.10 | async-start | bytes 9437184 | tf_op jit(solution)/shard_map/reduce_scatter | solution.py:87
  48.4 42.4 %all-to-all-start.2 = ((bf16[32,2,8192]{2,1,0:T(2,128)(2,1)}), bf16[32,2,8192]{2,1,0:T(2,128)(2,1)}, u32[]{:S(2)}, u32[]{:S(2)}) async-start(bf16[32,2,8192]{2,1,0:T(2,128)(2,1)} %reshape.139), calls=%async_computation.2 | async-start | bytes 2097152 | tf_op jit(solution)/shard_map/all_to_all | solution.py:72
  90.8 40.5 %all-to-all-start = ((bf16[32,2,8192]{2,1,0:T(2,128)(2,1)}), bf16[32,2,8192]{2,1,0:T(2,128)(2,1)}, u32[]{:S(2)}, u32[]{:S(2)}) async-start(bf16[32,2,8192]{2,1,0:T(2,128)(2,1)} %reshape.141), calls=%async_computation | async-start | bytes 2097152 | tf_op jit(solution)/shard_map/all_to_all | solution.py:71
  131.4 124.7 %all-to-all-start.1 = ((bf16[32,2,8192]{2,1,0:T(2,128)(2,1)}), bf16[32,2,8192]{2,1,0:T(2,128)(2,1)}, u32[]{:S(2)}, u32[]{:S(2)}) async-start(bf16[32,2,8192]{2,1,0:T(2,128)(2,1)} %reshape.143), calls=%async_computation.1 | async-start | bytes 2097152 | tf_op jit(solution)/shard_map/all_to_all | solution.py:70
  230.5 35.4 %copy-start.4 = (s32[64,4]{0,1:T(4,128)S(1)}, s32[64,4]{0,1:T(4,128)}, u32[]{:S(2)}) copy-start(s32[64,4]{0,1:T(4,128)} %param.11) | copy-start | bytes 3076
  256.1 49.0 %all-to-all-start.4 = ((bf16[32,2,8192]{2,1,0:T(2,128)(2,1)}), bf16[32,2,8192]{2,1,0:T(2,128)(2,1)}, u32[]{:S(2)}, u32[]{:S(2)}) async-start(bf16[32,2,8192]{2,1,0:T(2,128)(2,1)} %reshape.147), calls=%async_computation.5 | async-start | bytes 2097152 | tf_op jit(solution)/shard_map/all_to_all | solution.py:95
  265.9 317.8 %all-gather.2.cloned.1.call-start = ((), (), s32[]{:S(2)}) async-start(), calls=%async_computation.11 | async-start | bytes 9437184 | tf_op jit(solution)/shard_map/all_gather | solution.py:114
  300.2 2.0 copy-start.2
  417.7 444.9 %reduce-scatter.5.cloned.1.call-start = ((), (), s32[]{:S(2)}) async-start(), calls=%async_computation.12 | async-start | bytes 4325376 | tf_op jit(solution)/shard_map/reduce_scatter | solution.py:115
  638.8 83.5 %all-to-all-start.5 = ((bf16[32,2,8192]{2,1,0:T(2,128)(2,1)}), bf16[32,2,8192]{2,1,0:T(2,128)(2,1)}, u32[]{:S(2)}, u32[]{:S(2)}) async-start(bf16[32,2,8192]{2,1,0:T(2,128)(2,1)} %reshape.149), calls=%async_computation.6 | async-start | bytes 2097152 | tf_op jit(solution)/shard_map/all_to_all | solution.py:110
  721.2 11.4 %copy-start.3 = (bf16[1,32,128,128]{3,2,1,0:T(8,128)(2,1)S(1)}, bf16[1,32,128,128]{3,2,1,0:T(8,128)(2,1)}, u32[]{:S(2)}) copy-start(bf16[1,32,128,128]{3,2,1,0:T(8,128)(2,1)} %copy.86) | copy-start | bytes 3145732
  722.3 91.4 %all-to-all-start.6 = ((bf16[32,2,8192]{2,1,0:T(2,128)(2,1)}), bf16[32,2,8192]{2,1,0:T(2,128)(2,1)}, u32[]{:S(2)}, u32[]{:S(2)}) async-start(bf16[32,2,8192]{2,1,0:T(2,128)(2,1)} %reshape.151), calls=%async_computation.7 | async-start | bytes 2097152 | tf_op jit(solution)/shard_map/all_to_all | solution.py:111
  813.7 40.4 %all-to-all-start.7 = ((bf16[32,2,8192]{2,1,0:T(2,128)(2,1)}), bf16[32,2,8192]{2,1,0:T(2,128)(2,1)}, u32[]{:S(2)}, u32[]{:S(2)}) async-start(bf16[32,2,8192]{2,1,0:T(2,128)(2,1)} %reshape.153), calls=%async_computation.8 | async-start | bytes 2097152 | tf_op jit(solution)/shard_map/all_to_all | solution.py:112
  854.1 10.1 %copy-start.1 = (bf16[8,128,512]{2,1,0:T(8,128)(2,1)S(1)}, bf16[8,128,512]{2,1,0:T(8,128)(2,1)}, u32[]{:S(2)}) copy-start(bf16[8,128,512]{2,1,0:T(8,128)(2,1)} %param.9) | copy-start | bytes 3145732
Sparse Core Ops, SparseCore 0:
  17.5 208.0 reduce-scatter.2
  417.8 165.8 all-gather.1
  593.6 137.1 reduce-scatter.4
where the time goes:
time: 881 us; the launch traced here: 871 us
  waiting for transfers between devices  260 us (30%)
  other arithmetic  243 us (28%)
  local copies, waits for them, and re-layouts  175 us (20%)
  starting transfers between devices  72.2 us (8%)
  matrix products  66.5 us (8%)
  blocking collectives  40.3 us (5%)
  between operations  14.6 us (2%)
    unnamed x8, other arithmetic  185 us
    all_gather x1, waiting for transfers between devices, on_device(): every_sequence = lax.all_gather(attended, 'tp', axis=0, tiled=True)  159 us
    unnamed x43, local copies, waits for them, and re-layouts  84.4 us
    reduce_scatter x1, waiting for transfers between devices, on_device(): lax.psum_scatter(jnp.einsum('stc,dc->std', upstream, out_weight, preferre...  84 us
    another operation x4, local copies, waits for them, and re-layouts, join_heads(): return array.reshape(count_heads, length, HD).transpose(1, 0, 2).reshape(...  68 us
    all_to_all x1, blocking collectives, on_device(): lax.all_to_all(join_heads(results[0]), 'seq', split_axis=1, concat_axis=2...  40.3 us
    scatter-add x1, other arithmetic, backward_head(): key_grad = jnp.zeros((block_count, BLK, HD), jnp.float32).at[flat_list].a...  26.3 us
    scatter-add x1, other arithmetic, backward_head(): value_grad = jnp.zeros((block_count, BLK, HD), jnp.float32).at[flat_list]...  26.2 us
  transfers between devices with their start and end apart: 10, of which 4 were waited for; matrix products, arithmetic and copies ran while one was open for 45% of the time, Pallas kernels for 0%

commit v1 on v0

--- a/solution.py
+++ b/solution.py
@@ -7,6 +7,19 @@
 HD = 128
 BLK = 64
 NB = 4
+
+
+def spots_post(mat):
+    met_up = jnp.concatenate(
+        lax.all_to_all(
+            jnp.stack(jnp.split(mat, lax.axis_size("seq"), axis=1)),
+            "seq",
+            split_axis=0,
+            concat_axis=0,
+        ),
+        axis=2,
+    )
+    return met_up
 
 
 def forward_head(query_rows, key_rows, value_rows, blocks):
@@ -106,7 +119,7 @@
 
     results = lax.map(both_one, stacked)
     attended, query_grad, key_grad, value_grad = (
-        lax.all_to_all(join_heads(results[0]), "seq", split_axis=1, concat_axis=2, tiled=True),
+        spots_post(join_heads(results[0])),
         lax.all_to_all(join_heads(results[1]), "seq", split_axis=1, concat_axis=2, tiled=True),
         lax.all_to_all(join_heads(results[2]), "seq", split_axis=1, concat_axis=2, tiled=True),
         lax.all_to_all(join_heads(results[3]), "seq", split_axis=1, concat_axis=2, tiled=True),

time: 881 us -> 832 us (0.944)
  local copies, waits for them, and re-layouts: 175 us -> 149 us
  other arithmetic: 243 us -> 219 us
    unnamed x8 -> x7, other arithmetic: 185 us -> 162 us
    another operation x4 -> x3, local copies, waits for them, and re-layouts: 68 us -> 50.5 us  [join_heads(): return array.reshape(count_heads, length, HD).transpose(1, 0, 2).reshape(...]
    unnamed x43 -> x72, local copies, waits for them, and re-layouts: 84.4 us -> 76.2 us
  transfers between devices with their start and end apart: 10 -> 10, of which waited for: 4 -> 4; matrix products, arithmetic and copies ran while one was open for 45% -> 47% of each run, Pallas kernels for 0% -> 0%
where the time goes in v1:
time: 832 us; the launch traced here: 822 us
  waiting for transfers between devices  261 us (31%)
  other arithmetic  219 us (26%)
  local copies, waits for them, and re-layouts  149 us (18%)
  starting transfers between devices  72.1 us (9%)
  matrix products  66.2 us (8%)
  blocking collectives  40.4 us (5%)
  between operations  14.7 us (2%)
    unnamed x7, other arithmetic  162 us
    all_gather x1, waiting for transfers between devices, on_device(): every_sequence = lax.all_gather(attended, 'tp', axis=0, tiled=True)  159 us
    reduce_scatter x1, waiting for transfers between devices, on_device(): lax.psum_scatter(jnp.einsum('stc,dc->std', upstream, out_weight, preferre...  84.1 us
    unnamed x72, local copies, waits for them, and re-layouts  76.2 us
    another operation x3, local copies, waits for them, and re-layouts, join_heads(): return array.reshape(count_heads, length, HD).transpose(1, 0, 2).reshape(...  50.5 us
    all_to_all x1, blocking collectives, spots_post(): lax.all_to_all(jnp.stack(jnp.split(mat, lax.axis_size('seq'), axis=1)), '...  40.4 us
    scatter-add x1, other arithmetic, backward_head(): key_grad = jnp.zeros((block_count, BLK, HD), jnp.float32).at[flat_list].a...  26.3 us
    scatter-add x1, other arithmetic, backward_head(): value_grad = jnp.zeros((block_count, BLK, HD), jnp.float32).at[flat_list]...  26.2 us
  transfers between devices with their start and end apart: 10, of which 4 were waited for; matrix products, arithmetic and copies ran while one was open for 47% of the time, Pallas kernels for 0%

profile of v1, /device:TPU:32, one launch (start us, length us, event | category | flops | bytes accessed | tf_op | source)
XLA Modules:
  0.0 822.1 jit_solution(14633177357248879832)
XLA Ops:
  22.9 23.4 %reduce.1 = bf16[4096,128]{1,0:T(8,128)(2,1)} reduce(bf16[4096,1,128]{2,1,0:T(2,128)(2,1)S(1)} %bitcast.255, bf16[]{:T(256)} %broadcast.81), dimensions={1}, to_apply=%bitcast.199.reduce_sub_computation | reduce | bytes 2097154
  48.4 11.6 %all-to-all-start.2 = ((bf16[32,2,8192]{2,1,0:T(2,128)(2,1)}), bf16[32,2,8192]{2,1,0:T(2,128)(2,1)}, u32[]{:S(2)}, u32[]{:S(2)}) async-start(bf16[32,2,8192]{2,1,0:T(2,128)(2,1)} %reshape.147), calls=%async_computation.2 | async-start | bytes 2097152 | tf_op jit(solution)/shard_map/all_to_all | solution.py:85
  65.1 23.4 %reduce.2 = bf16[4096,128]{1,0:T(8,128)(2,1)} reduce(bf16[4096,1,128]{2,1,0:T(2,128)(2,1)S(1)} %bitcast.260, bf16[]{:T(256)} %broadcast.81), dimensions={1}, to_apply=%bitcast.201.reduce_sub_computation | reduce | bytes 2097154
  90.6 9.9 %all-to-all-start = ((bf16[32,2,8192]{2,1,0:T(2,128)(2,1)}), bf16[32,2,8192]{2,1,0:T(2,128)(2,1)}, u32[]{:S(2)}, u32[]{:S(2)}) async-start(bf16[32,2,8192]{2,1,0:T(2,128)(2,1)} %reshape.149), calls=%async_computation | async-start | bytes 2097152 | tf_op jit(solution)/shard_map/all_to_all | solution.py:84
  105.5 23.4 %reduce.3 = bf16[4096,128]{1,0:T(8,128)(2,1)} reduce(bf16[4096,1,128]{2,1,0:T(2,128)(2,1)S(1)} %bitcast.261, bf16[]{:T(256)} %broadcast.81), dimensions={1}, to_apply=%bitcast.203.reduce_sub_computation | reduce | bytes 2097154
  131.1 10.3 %all-to-all-start.1 = ((bf16[32,2,8192]{2,1,0:T(2,128)(2,1)}), bf16[32,2,8192]{2,1,0:T(2,128)(2,1)}, u32[]{:S(2)}, u32[]{:S(2)}) async-start(bf16[32,2,8192]{2,1,0:T(2,128)(2,1)} %reshape.151), calls=%async_computation.1 | async-start | bytes 2097152 | tf_op jit(solution)/shard_map/all_to_all | solution.py:83
  141.5 84.1 %reduce-scatter.3.cloned.1.call-done = bf16[1,128,4096]{2,1,0:T(8,128)(2,1)} async-done(((bf16[8,128,4096]{2,1,0:T(8,128)(2,1)}), bf16[1,128,4096]{2,1,0:T(8,128)(2,1)}) %reduce-scatter.3.cloned.1.call-update) | async-done | bytes 1048592 | tf_op jit(solution)/shard_map/reduce_scatter | solution.py:100
  230.6 23.4 %reduce = bf16[4096,128]{1,0:T(8,128)(2,1)} reduce(bf16[4096,1,128]{2,1,0:T(2,128)(2,1)S(1)} %bitcast.257, bf16[]{:T(256)} %broadcast.81), dimensions={1}, to_apply=%bitcast.205.reduce_sub_computation | reduce | bytes 2097154
  313.8 12.7 %multiply_reduce_fusion = (f32[64,64]{1,0:T(8,128)S(1)}, bf16[64,64,128]{2,1,0:T(8,128)(2,1)S(1)}) fusion(bf16[64,64,128]{2,1,0:T(8,128)(2,1)} %bitcast.309, bf16[64,256,128]{2,1,0:T(8,128)(2,1)} %bitcast.272, f32[64,64]{1,0:T(8,128)S(1)} %get-tuple-element.65, f32[64,256,64]{1,2,0:T(8,128)} %copy-done.2), kind=kOutput, calls=%fused_computation.14 | convolution fusion | flops 276300032 | bytes 10518528 | tf_op jit(solution)/shard_map/while/body/eval_jaxpr/qij,qjd->qid/dot_general | solution.py:39
  327.0 40.4 %all_to_all.119 = bf16[32,1,128,128]{3,2,1,0:T(8,128)(2,1)S(1)} all-to-all(bf16[32,1,128,128]{3,2,1,0:T(8,128)(2,1)S(1)} %constant_dynamic-update-slice_fusion), channel_id=1, replica_groups=mesh['seq'=32,'tp'=8] {'seq'}, dimensions={0} | all-to-all | bytes 2097152 | tf_op jit(solution)/shard_map/all_to_all | solution.py:14
  375.7 158.9 %all-gather.2.cloned.1.call-done = bf16[8,128,4096]{2,1,0:T(8,128)(2,1)} async-done(((bf16[1,128,4096]{2,1,0:T(8,128)(2,1)}), bf16[8,128,4096]{2,1,0:T(8,128)(2,1)}) %all-gather.2.cloned.1.call-update) | async-done | bytes 8388624 | tf_op jit(solution)/shard_map/all_gather | solution.py:127
  548.1 17.1 %copy.111 = bf16[1,4096,128]{2,0,1:T(2,128)(2,1)} copy(bf16[1,4096,128]{2,1,0:T(8,128)(2,1)S(1)} %bitcast.262) | data formatting | bytes 2097152 | tf_op jit(solution)/shard_map/reshape;transpose;reshape | solution.py:97
  565.2 23.5 %reduce.4 = bf16[4096,128]{1,0:T(8,128)(2,1)S(1)} reduce(bf16[4096,1,128]{2,1,0:T(2,128)(2,1)} %bitcast.258, bf16[]{:T(256)} %broadcast.81), dimensions={1}, to_apply=%bitcast.239.reduce_sub_computation | reduce | bytes 2097154
  589.7 10.2 %all-to-all-start.5 = ((bf16[32,2,8192]{2,1,0:T(2,128)(2,1)}), bf16[32,2,8192]{2,1,0:T(2,128)(2,1)}, u32[]{:S(2)}, u32[]{:S(2)}) async-start(bf16[32,2,8192]{2,1,0:T(2,128)(2,1)} %reshape.155), calls=%async_computation.6 | async-start | bytes 2097152 | tf_op jit(solution)/shard_map/all_to_all | solution.py:123
  606.5 26.3 %scatter_fusion = f32[64,64,128]{2,1,0:T(8,128)S(1)} fusion(f32[64,64,128]{2,1,0:T(8,128)S(1)} %broadcast.50.clone, s32[256]{0:T(256)S(1)} %bitcast.312, f32[256,64,128]{2,1,0:T(8,128)} %bitcast.242), kind=kCustom, calls=%fused_computation.2 | custom fusion | flops 2097152 | bytes 25166848 | tf_op jit(solution)/shard_map/while/body/eval_jaxpr/scatter-add | solution.py:69
  633.0 16.7 %copy.110 = bf16[1,4096,128]{2,0,1:T(2,128)(2,1)S(1)} copy(bf16[1,4096,128]{2,1,0:T(8,128)(2,1)S(1)} %bitcast.263) | data formatting | bytes 2097152 | tf_op jit(solution)/shard_map/reshape;transpose;reshape | solution.py:97
  649.7 22.4 %reduce.5 = bf16[4096,128]{1,0:T(8,128)(2,1)S(1)} reduce(bf16[4096,1,128]{2,1,0:T(2,128)(2,1)S(1)} %bitcast.259, bf16[]{:T(256)} %broadcast.81), dimensions={1}, to_apply=%bitcast.238.reduce_sub_computation | reduce | bytes 2097154
  673.2 10.3 %all-to-all-start.6 = ((bf16[32,2,8192]{2,1,0:T(2,128)(2,1)}), bf16[32,2,8192]{2,1,0:T(2,128)(2,1)}, u32[]{:S(2)}, u32[]{:S(2)}) async-start(bf16[32,2,8192]{2,1,0:T(2,128)(2,1)} %reshape.157), calls=%async_computation.7 | async-start | bytes 2097152 | tf_op jit(solution)/shard_map/all_to_all | solution.py:124
  683.6 14.2 %fusion.10 = f32[64,256,128]{2,1,0:T(8,128)} fusion(bf16[64,64,128]{2,1,0:T(8,128)(2,1)S(1)} %bitcast.311, f32[64,64]{1,0:T(8,128)S(1)} %get-tuple-element.65, f32[64,256,64]{1,2,0:T(8,128)} %copy-done.2), kind=kOutput, calls=%fused_computation.89 | convolution fusion | flops 273682688 | bytes 13647872 | tf_op jit(solution)/shard_map/while/body/eval_jaxpr/qij,qid->qjd/dot_general | solution.py:63
  698.0 26.2 %scatter_fusion.1 = f32[64,64,128]{2,1,0:T(8,128)S(1)} fusion(f32[64,64,128]{2,1,0:T(8,128)S(1)} %broadcast.50.clone.1, s32[256]{0:T(256)S(1)} %bitcast.313, f32[256,64,128]{2,1,0:T(8,128)} %bitcast.254), kind=kCustom, calls=%fused_computation.3 | custom fusion | flops 2097152 | bytes 25166848 | tf_op jit(solution)/shard_map/while/body/eval_jaxpr/scatter-add | solution.py:75
  724.4 16.7 %copy.109 = bf16[1,4096,128]{2,0,1:T(2,128)(2,1)S(1)} copy(bf16[1,4096,128]{2,1,0:T(8,128)(2,1)S(1)} %bitcast.264) | data formatting | bytes 2097152 | tf_op jit(solution)/shard_map/reshape;transpose;reshape | solution.py:97
  741.1 22.4 %reduce.6 = bf16[4096,128]{1,0:T(8,128)(2,1)S(1)} reduce(bf16[4096,1,128]{2,1,0:T(2,128)(2,1)S(1)} %bitcast.256, bf16[]{:T(256)} %broadcast.81), dimensions={1}, to_apply=%bitcast.237.reduce_sub_computation | reduce | bytes 2097154
  764.7 9.9 %all-to-all-start.7 = ((bf16[32,2,8192]{2,1,0:T(2,128)(2,1)}), bf16[32,2,8192]{2,1,0:T(2,128)(2,1)}, u32[]{:S(2)}, u32[]{:S(2)}) async-start(bf16[32,2,8192]{2,1,0:T(2,128)(2,1)} %reshape.159), calls=%async_computation.8 | async-start | bytes 2097152 | tf_op jit(solution)/shard_map/all_to_all | solution.py:125
  787.4 17.7 %all-to-all-done.7 = bf16[32,2,8192]{2,1,0:T(2,128)(2,1)} async-done(((bf16[32,2,8192]{2,1,0:T(2,128)(2,1)}), bf16[32,2,8192]{2,1,0:T(2,128)(2,1)}, u32[]{:S(2)}, u32[]{:S(2)}) %all-to-all-start.7) | async-done | bytes 1048608 | tf_op jit(solution)/shard_map/all_to_all | solution.py:125
  (116 shorter events, 152.6 us)
Async XLA Ops:
  7.2 1.2 copy-start
  7.2 218.3 %reduce-scatter.3.cloned.1.call-start = ((), (), s32[]{:S(2)}) async-start(), calls=%async_computation.10 | async-start | bytes 9437184 | tf_op jit(solution)/shard_map/reduce_scatter | solution.py:100
  48.4 42.2 %all-to-all-start.2 = ((bf16[32,2,8192]{2,1,0:T(2,128)(2,1)}), bf16[32,2,8192]{2,1,0:T(2,128)(2,1)}, u32[]{:S(2)}, u32[]{:S(2)}) async-start(bf16[32,2,8192]{2,1,0:T(2,128)(2,1)} %reshape.147), calls=%async_computation.2 | async-start | bytes 2097152 | tf_op jit(solution)/shard_map/all_to_all | solution.py:85
  90.6 40.5 %all-to-all-start = ((bf16[32,2,8192]{2,1,0:T(2,128)(2,1)}), bf16[32,2,8192]{2,1,0:T(2,128)(2,1)}, u32[]{:S(2)}, u32[]{:S(2)}) async-start(bf16[32,2,8192]{2,1,0:T(2,128)(2,1)} %reshape.149), calls=%async_computation | async-start | bytes 2097152 | tf_op jit(solution)/shard_map/all_to_all | solution.py:84
  131.1 125.0 %all-to-all-start.1 = ((bf16[32,2,8192]{2,1,0:T(2,128)(2,1)}), bf16[32,2,8192]{2,1,0:T(2,128)(2,1)}, u32[]{:S(2)}, u32[]{:S(2)}) async-start(bf16[32,2,8192]{2,1,0:T(2,128)(2,1)} %reshape.151), calls=%async_computation.1 | async-start | bytes 2097152 | tf_op jit(solution)/shard_map/all_to_all | solution.py:83
  230.5 35.4 %copy-start.5 = (s32[64,4]{0,1:T(4,128)S(1)}, s32[64,4]{0,1:T(4,128)}, u32[]{:S(2)}) copy-start(s32[64,4]{0,1:T(4,128)} %param.11) | copy-start | bytes 3076
  256.1 48.9 %all-to-all-start.4 = ((bf16[32,2,8192]{2,1,0:T(2,128)(2,1)}), bf16[32,2,8192]{2,1,0:T(2,128)(2,1)}, u32[]{:S(2)}, u32[]{:S(2)}) async-start(bf16[32,2,8192]{2,1,0:T(2,128)(2,1)} %reshape.153), calls=%async_computation.5 | async-start | bytes 2097152 | tf_op jit(solution)/shard_map/all_to_all | solution.py:108
  265.9 268.8 %all-gather.2.cloned.1.call-start = ((), (), s32[]{:S(2)}) async-start(), calls=%async_computation.11 | async-start | bytes 9437184 | tf_op jit(solution)/shard_map/all_gather | solution.py:127
  300.2 2.0 copy-start.2
  327.0 41.6 %copy-start.3 = (bf16[1,32,128,128]{3,2,1,0:T(8,128)(2,1)S(1)}, bf16[1,32,128,128]{3,2,1,0:T(8,128)(2,1)}, u32[]{:S(2)}) copy-start(bf16[1,32,128,128]{3,2,1,0:T(8,128)(2,1)} %copy.84) | copy-start | bytes 3145732
  368.6 445.0 %reduce-scatter.5.cloned.1.call-start = ((), (), s32[]{:S(2)}) async-start(), calls=%async_computation.12 | async-start | bytes 4325376 | tf_op jit(solution)/shard_map/reduce_scatter | solution.py:128
  589.7 83.5 %all-to-all-start.5 = ((bf16[32,2,8192]{2,1,0:T(2,128)(2,1)}), bf16[32,2,8192]{2,1,0:T(2,128)(2,1)}, u32[]{:S(2)}, u32[]{:S(2)}) async-start(bf16[32,2,8192]{2,1,0:T(2,128)(2,1)} %reshape.155), calls=%async_computation.6 | async-start | bytes 2097152 | tf_op jit(solution)/shard_map/all_to_all | solution.py:123
  672.1 11.4 %copy-start.4 = (bf16[1,32,128,128]{3,2,1,0:T(8,128)(2,1)S(1)}, bf16[1,32,128,128]{3,2,1,0:T(8,128)(2,1)}, u32[]{:S(2)}) copy-start(bf16[1,32,128,128]{3,2,1,0:T(8,128)(2,1)} %copy.84) | copy-start | bytes 3145732
  673.2 91.4 %all-to-all-start.6 = ((bf16[32,2,8192]{2,1,0:T(2,128)(2,1)}), bf16[32,2,8192]{2,1,0:T(2,128)(2,1)}, u32[]{:S(2)}, u32[]{:S(2)}) async-start(bf16[32,2,8192]{2,1,0:T(2,128)(2,1)} %reshape.157), calls=%async_computation.7 | async-start | bytes 2097152 | tf_op jit(solution)/shard_map/all_to_all | solution.py:124
  764.7 40.4 %all-to-all-start.7 = ((bf16[32,2,8192]{2,1,0:T(2,128)(2,1)}), bf16[32,2,8192]{2,1,0:T(2,128)(2,1)}, u32[]{:S(2)}, u32[]{:S(2)}) async-start(bf16[32,2,8192]{2,1,0:T(2,128)(2,1)} %reshape.159), calls=%async_computation.8 | async-start | bytes 2097152 | tf_op jit(solution)/shard_map/all_to_all | solution.py:125
  805.1 10.1 %copy-start.1 = (bf16[8,128,512]{2,1,0:T(8,128)(2,1)S(1)}, bf16[8,128,512]{2,1,0:T(8,128)(2,1)}, u32[]{:S(2)}) copy-start(bf16[8,128,512]{2,1,0:T(8,128)(2,1)} %param.9) | copy-start | bytes 3145732
Sparse Core Ops, SparseCore 0:
  17.5 208.0 reduce-scatter.2
  368.7 165.9 all-gather.1
  544.5 137.2 reduce-scatter.4
